TPU v7x, 256 devices: a whole 4x4x8 slice. The times are simulated.
256 devices in a mesh: gx: 16 (over z, core), gy: 8 (over y_hi, x), ga: 2 (over y_lo).
Axes of the slice: x: 4, y: 4 (y_hi: 2, y_lo: 2; y = y_hi * 2 + y_lo), z: 8, core: 2. Of those that a mesh axis runs over, the one named last changes fastest.
Arguments:
- samples: bfloat16 [16, 128, 128, 512], P('ga', 'gx', 'gy'), parts along dimension 0, may hold values from -6 to 6
- model_prev: bfloat16 [16, 128, 128, 512], P('ga', 'gx', 'gy'), parts along dimension 0, may hold values from -6 to 6
- threshold: float32 [128, 128], P('gx', 'gy'), may hold values from 0.1 to 1
- support: int32 [128, 128, 256], P('gx', 'gy'), may hold values from 0 to 511
- sample_basis: bfloat16 [512, 64], replicated, may hold values from -0.25 to 0.25
- eval_basis: bfloat16 [64, 512], replicated, may hold values from -0.25 to 0.25
- transfer_x: bfloat16 [16, 16, 64, 64], replicated, may hold values from -0.1875 to 0.1875
- transfer_y: bfloat16 [8, 8, 64, 64], replicated, may hold values from -0.25 to 0.25
Outputs:
- model_next: float32 [16, 128, 128, 512], P('ga', 'gx', 'gy'), parts along dimension 0
- residual: bfloat16 [16, 128, 128, 512], P('ga', 'gx', 'gy'), parts along dimension 0
There are 2 independent parts, one for each index of `ga`. A program takes and returns all parts, laid end to end along the dimension named above; an argument that names none is the same for every part. Nothing has to cross between parts.
All inputs are finite; a program needn't handle non-finite values.
Results may differ from a plain program's by a relative error of at most 0.015.
Values may be sent and summed in bfloat16 or wider, within the bound.
A program may use at most 64 MiB of HBM per device.

v0:
```python
import jax
import jax.numpy as jnp
from jax import lax
from jax.sharding import PartitionSpec as P


def mix_terms(coeffs, column):
    row_count = coeffs.shape[0] * coeffs.shape[1]

    def term(offset, extent):
        box_count = extent // row_count
        produced = jnp.einsum("glmk,akq->aglmq", coeffs, column, preferred_element_type=jnp.float32)
        return produced.reshape(box_count * row_count, coeffs.shape[2] * column.shape[-1])

    return (term, row_count)


def level_x(coeffs, tables):
    own_index = lax.axis_index("gx")
    shape_out = (coeffs.shape[0], coeffs.shape[1], coeffs.shape[2], tables.shape[-1])
    column = lax.dynamic_index_in_dim(tables, own_index, 1, keepdims=False)
    term, row_count = mix_terms(coeffs, column)
    summed = lax.psum_scatter(
        term(jnp.int32(0), row_count * lax.axis_size("gx")).astype(jnp.bfloat16),
        "gx",
        scatter_dimension=0,
        tiled=True,
    ).astype(jnp.float32)
    return summed.reshape(shape_out)


def level_y(coeffs, tables):
    own_index = lax.axis_index("gy")
    shape_out = (coeffs.shape[0], coeffs.shape[1], coeffs.shape[2], tables.shape[-1])
    column = lax.dynamic_index_in_dim(tables, own_index, 1, keepdims=False)
    swapped = jnp.transpose(coeffs, (0, 2, 1, 3))
    term, row_count = mix_terms(swapped, column)
    summed = lax.psum_scatter(
        term(jnp.int32(0), lax.axis_size("gy") * row_count), "gy", scatter_dimension=0, tiled=True
    )
    return jnp.transpose(
        summed.reshape(shape_out[0], shape_out[2], shape_out[1], shape_out[3]), (0, 2, 1, 3)
    )


def on_device(
    samples, model_prev, threshold, support, sample_basis, eval_basis, transfer_x, transfer_y
):
    flipped_x = jnp.transpose(transfer_x, (1, 0, 3, 2))
    flipped_y = jnp.transpose(transfer_y, (1, 0, 3, 2))
    top = jnp.einsum(
        "glmr,kr->glmk", model_prev, eval_basis, preferred_element_type=jnp.float32
    ).astype(jnp.bfloat16)
    middle = level_y(top, flipped_y).astype(jnp.bfloat16)
    low = level_x(middle, flipped_x).astype(jnp.bfloat16)
    predicted = jnp.einsum("glmk,tk->glmt", low, sample_basis, preferred_element_type=jnp.float32)
    residual = (samples.astype(jnp.float32) - predicted).astype(jnp.bfloat16)
    back_low = jnp.einsum(
        "glmt,tk->glmk", residual, sample_basis, preferred_element_type=jnp.float32
    ).astype(jnp.bfloat16)
    back_mid = level_x(back_low, transfer_x).astype(jnp.bfloat16)
    back_top = level_y(back_mid, transfer_y).astype(jnp.bfloat16)
    update = jnp.einsum("glmk,kr->glmr", back_top, eval_basis, preferred_element_type=jnp.float32)
    stepped = model_prev.astype(jnp.float32) + update
    shrunk = jnp.sign(stepped) * jnp.maximum(jnp.abs(stepped) - threshold[None, :, :, None], 0.0)
    sample_slots = jnp.arange(model_prev.shape[3], dtype=jnp.int32)
    support_mask = jnp.any(
        support[:, :, :, None] == sample_slots[None, None, None, :], axis=2
    ).astype(jnp.float32)
    return (shrunk * support_mask[None], residual)


def solution(mesh):
    return jax.shard_map(
        on_device,
        mesh=mesh,
        in_specs=(
            P("ga", "gx", "gy", None),
            P("ga", "gx", "gy", None),
            P("gx", "gy"),
            P("gx", "gy", None),
            P(),
            P(),
            P(),
            P(),
        ),
        out_specs=(P("ga", "gx", "gy", None), P("ga", "gx", "gy", None)),
        check_vma=False,
    )
```

profile of v0, /device:TPU:1, one launch (start us, length us, event | category | flops | bytes accessed | tf_op | source)
XLA Modules:
  0.0 346.9 jit_solution(2874110469218211879)
XLA Ops:
  7.2 0.0 reduce-scatter.5.cloned.1.call-start
  7.2 1.2 copy-done
  8.4 0.1 copy.31
  8.5 4.5 %convolution_bitcast_fusion.1 = f32[8,8,16,8,64]{4,2,3,1,0:T(8,128)} fusion(bf16[8,8,16,512]{3,2,1,0:T(8,128)(2,1)} %param.9, bf16[1,8,64,64]{2,3,1,0:T(8,128)(2,1)S(1)} %copy.31, bf16[64,512]{1,0:T(8,128)(2,1)} %param.13), kind=kOutput, calls=%fused_computation.5 | convolution fusion | flops 134283264 | bytes 3276800 | tf_op jit(solution)/shard_map/glmk,akq->aglmq/dot_general | solution.py:12
  13.0 6.1 %copy.20 = f32[8,8,16,8,64]{4,3,2,1,0:T(8,128)} copy(f32[8,8,16,8,64]{4,2,3,1,0:T(8,128)} %convolution_bitcast_fusion.1) | data formatting | bytes 4194304 | tf_op jit(solution)/shard_map/glmk,akq->aglmq/transpose | solution.py:12
  19.1 4.8 %reshape.27 = f32[1024,512]{1,0:T(8,128)} reshape(f32[8,8,16,8,64]{4,3,2,1,0:T(8,128)} %copy.20) | data formatting | bytes 4194304 | tf_op jit(solution)/shard_map/reshape | solution.py:13
  23.9 0.0 reduce-scatter.7.cloned.1.call-start
  24.0 1.0 constant_dynamic-slice_fusion.1
  25.0 0.2 copy.30
  25.2 81.7 %reduce-scatter.5.cloned.1.call-done = f32[128,512]{1,0:T(8,128)} async-done(((f32[1024,512]{1,0:T(8,128)}), f32[128,512]{1,0:T(8,128)}) %reduce-scatter.5.cloned.1.call-update) | async-done | bytes 262160 | tf_op jit(solution)/shard_map/reduce_scatter | solution.py:38
  106.9 1.0 convert_element_type.76
  107.9 0.2 convert_element_type.77
  108.0 3.2 convert_bitcast_fusion.1
  111.2 6.5 %convert_element_type.81 = bf16[1024,1024]{1,0:T(8,128)(2,1)} reshape(bf16[16,8,8,16,64]{4,3,2,1,0:T(8,128)(2,1)} %convert_bitcast_fusion.1) | data formatting | bytes 4194304 | tf_op jit(solution)/shard_map/convert_element_type | solution.py:24
  117.7 0.0 reduce-scatter.9.cloned.1.call-start
  117.8 56.8 %reduce-scatter.7.cloned.1.call-done = bf16[64,1024]{1,0:T(8,128)(2,1)} async-done(((bf16[1024,1024]{1,0:T(8,128)(2,1)}), bf16[64,1024]{1,0:T(8,128)(2,1)}) %reduce-scatter.7.cloned.1.call-update) | async-done | bytes 131088 | tf_op jit(solution)/shard_map/reduce_scatter | solution.py:23
  174.6 1.1 convert_element_type.82
  175.7 0.4 subtract_convert_fusion
  176.1 5.0 %convert_bitcast_fusion = bf16[16,8,8,16,64]{4,3,2,1,0:T(8,128)(2,1)} fusion(bf16[8,8,16,512]{3,2,1,0:T(8,128)(2,1)S(1)} %subtract_convert_fusion, bf16[16,16,64,64]{3,2,1,0:T(8,128)(2,1)} %param.14, s32[]{:T(128)S(6)} %select_n.11, bf16[512,64]{0,1:T(8,128)(2,1)S(1)} %copy-done.4), kind=kOutput, calls=%fused_computation.2 | convolution fusion | flops 202440704 | bytes 3473412 | tf_op jit(solution)/shard_map/glmk,akq->aglmq/dot_general | solution.py:12
  181.1 6.5 %convert_element_type.87 = bf16[1024,1024]{1,0:T(8,128)(2,1)} reshape(bf16[16,8,8,16,64]{4,3,2,1,0:T(8,128)(2,1)} %convert_bitcast_fusion) | data formatting | bytes 4194304 | tf_op jit(solution)/shard_map/convert_element_type | solution.py:24
  187.6 0.2 reduce-scatter.11.cloned.1.call-start
  187.9 57.7 %reduce-scatter.9.cloned.1.call-done = bf16[64,1024]{1,0:T(8,128)(2,1)} async-done(((bf16[1024,1024]{1,0:T(8,128)(2,1)}), bf16[64,1024]{1,0:T(8,128)(2,1)}) %reduce-scatter.9.cloned.1.call-update) | async-done | bytes 131088 | tf_op jit(solution)/shard_map/reduce_scatter | solution.py:23
  245.6 1.1 convert_element_type.88
  246.7 0.7 convolution_bitcast_fusion
  247.4 3.9 %copy.22 = f32[8,8,16,8,64]{4,3,2,1,0:T(8,128)} copy(f32[8,8,16,8,64]{4,2,3,1,0:T(8,128)S(1)} %convolution_bitcast_fusion) | data formatting | bytes 4194304 | tf_op jit(solution)/shard_map/glmk,akq->aglmq/transpose | solution.py:12
  251.3 4.8 %reshape.28 = f32[1024,512]{1,0:T(8,128)} reshape(f32[8,8,16,8,64]{4,3,2,1,0:T(8,128)} %copy.22) | data formatting | bytes 4194304 | tf_op jit(solution)/shard_map/reshape | solution.py:13
  256.1 0.9 copy-done.5
  257.0 12.5 %fusion = pred[8,16,512]{2,1,0:T(8,128)(4,1)S(1)} fusion(s32[8,16,256]{2,1,0:T(8,128)S(1)} %copy-done.5), kind=kLoop, calls=%fused_computation.1 | loop fusion | flops 33488896 | bytes 196608 | tf_op jit(solution)/shard_map/reduce_or | solution.py:67
  269.6 67.2 %reduce-scatter.11.cloned.1.call-done = f32[128,512]{1,0:T(8,128)} async-done(((f32[1024,512]{1,0:T(8,128)}), f32[128,512]{1,0:T(8,128)}) %reduce-scatter.11.cloned.1.call-update) | async-done | bytes 262160 | tf_op jit(solution)/shard_map/reduce_scatter | solution.py:38
  336.7 1.0 convert_element_type.89
  337.7 0.2 convert_element_type.90
  337.9 2.4 multiply_multiply_fusion
  (20 shorter events, 0.1 us)
Async XLA Ops:
  7.2 1.2 copy-start
  7.2 99.7 %reduce-scatter.5.cloned.1.call-start = ((), (), s32[]{:S(2)}) async-start(), calls=%async_computation.4 | async-start | bytes 2359296 | tf_op jit(solution)/shard_map/reduce_scatter | solution.py:38
  23.9 150.6 %reduce-scatter.7.cloned.1.call-start = ((), (), s32[]{:S(2)}) async-start(), calls=%async_computation.5 | async-start | bytes 2228224 | tf_op jit(solution)/shard_map/reduce_scatter | solution.py:23
  117.7 58.0 %copy-start.2 = (bf16[8,8,16,512]{3,2,1,0:T(8,128)(2,1)S(1)}, bf16[8,8,16,512]{3,2,1,0:T(8,128)(2,1)}, u32[]{:S(2)}) copy-start(bf16[8,8,16,512]{3,2,1,0:T(8,128)(2,1)} %param.8) | copy-start | bytes 3145732
  117.7 58.0 %copy-start.4 = (bf16[512,64]{0,1:T(8,128)(2,1)S(1)}, bf16[512,64]{0,1:T(8,128)(2,1)}, u32[]{:S(2)}) copy-start(bf16[512,64]{0,1:T(8,128)(2,1)} %param.12) | copy-start | bytes 196612
  117.7 127.9 %reduce-scatter.9.cloned.1.call-start = ((), (), s32[]{:S(2)}) async-start(), calls=%async_computation.6 | async-start | bytes 2228224 | tf_op jit(solution)/shard_map/reduce_scatter | solution.py:23
  176.1 5.0 %copy-start.1 = (bf16[8,8,16,512]{3,2,1,0:T(8,128)(2,1)}, bf16[8,8,16,512]{3,2,1,0:T(8,128)(2,1)S(1)}, u32[]{:S(2)}) copy-start(bf16[8,8,16,512]{3,2,1,0:T(8,128)(2,1)S(1)} %subtract_convert_fusion) | copy-start | bytes 3145732
  187.6 149.1 %reduce-scatter.11.cloned.1.call-start = ((), (), s32[]{:S(2)}) async-start(), calls=%async_computation.7 | async-start | bytes 2359296 | tf_op jit(solution)/shard_map/reduce_scatter | solution.py:38
  256.1 0.9 copy-start.5
  256.1 81.8 %copy-start.3 = (bf16[8,8,16,512]{3,2,1,0:T(8,128)(2,1)S(1)}, bf16[8,8,16,512]{3,2,1,0:T(8,128)(2,1)}, u32[]{:S(2)}) copy-start(bf16[8,8,16,512]{3,2,1,0:T(8,128)(2,1)} %param.9) | copy-start | bytes 3145732
  256.1 81.8 %copy-start.6 = (bf16[64,512]{1,0:T(8,128)(2,1)S(1)}, bf16[64,512]{1,0:T(8,128)(2,1)}, u32[]{:S(2)}) copy-start(bf16[64,512]{1,0:T(8,128)(2,1)} %param.13) | copy-start | bytes 196612
  256.1 81.9 %copy-start.7 = (f32[8,16]{1,0:T(8,128)S(1)}, f32[8,16]{1,0:T(8,128)}, u32[]{:S(2)}) copy-start(f32[8,16]{1,0:T(8,128)} %param.10) | copy-start | bytes 1540
Sparse Core Ops, SparseCore 0:
  24.1 82.7 reduce-scatter.4
  117.8 56.6 reduce-scatter.6
  187.8 57.7 reduce-scatter.8
  256.2 80.4 reduce-scatter.10
where the time goes:
time: 348 us; the launch traced here: 347 us
  waiting for transfers between devices  264 us (76%)
  local copies, waits for them, and re-layouts  38.5 us (11%)
  matrix products  16.1 us (5%)
  other arithmetic  14.5 us (4%)
  between operations  13.9 us (4%)
    reduce_scatter x2, waiting for transfers between devices, level_y(): lax.psum_scatter(term(jnp.int32(0), lax.axis_size('gy') * row_count), 'gy...  149 us
    reduce_scatter x2, waiting for transfers between devices, level_x(): lax.psum_scatter(term(jnp.int32(0), row_count * lax.axis_size('gx')).asty...  115 us
    dot_general x4, matrix products, term(): jnp.einsum('glmk,akq->aglmq', coeffs, column, preferred_element_type=jnp....  13.3 us
    convert_element_type x2, local copies, waits for them, and re-layouts, level_x(): term(jnp.int32(0), row_count * lax.axis_size('gx')).astype(jnp.bfloat16)  13 us
    reduce_or x1, other arithmetic, on_device(): jnp.any(support[:, :, :, None] == sample_slots[None, None, None, :], axis=2)  12.5 us
    transpose x2, local copies, waits for them, and re-layouts, term(): jnp.einsum('glmk,akq->aglmq', coeffs, column, preferred_element_type=jnp....  10 us
    reshape x2, local copies, waits for them, and re-layouts, term(): produced.reshape(box_count * row_count, coeffs.shape[2] * column.shape[-1])  9.54 us
  transfers between devices with their start and end apart: 4, of which 4 were waited for; matrix products, arithmetic and copies ran while one was open for 4% of the time, Pallas kernels for 0%

commit v1 on v0

v1 whole, which is shorter than its diff:
```python
import functools

import jax
import jax.numpy as jnp
from jax import lax
from jax.experimental import pallas as pl
from jax.experimental.pallas import tpu as pltpu
from jax.sharding import PartitionSpec as P

BF = jnp.bfloat16
F32 = jnp.float32
MESH = pl.DeviceIdType.MESH
NX, NY = 16, 8
LAST = (((1,), (1,)), ((), ()))
PLAIN = (((1,), (0,)), ((), ()))


def dot(a, b, dims=PLAIN):
    return lax.dot_general(a, b, dims, preferred_element_type=F32)


def halves(u, v):
    return (
        jnp.concatenate([u[:, :64], v[:, :64]], axis=1),
        jnp.concatenate([u[:, 64:], v[:, 64:]], axis=1),
    )


def kernel(
    samples, model, thr, sup, sb, eb, tx, ty,
    out_model, out_res,
    m_v, s_v, tx_v, ty_v, bx, by, sb_v, eb_v, sl, sh, ea, ez, sup_v, supt, bits, thr_v, teff,
    res_v, om_v,
    s1, s2, s3, s4, s5, s6, r1, r2, r3, r4, r5, r6,
    in_sem, out_sem, send_sem, recv_sem,
):
    gx, gy = lax.axis_index("gx"), lax.axis_index("gy")
    half, owner = lax.rem(gx, 2), gx // 2
    own = owner == gy

    loads = [
        (model, m_v), (eb, eb_v), (ty, ty_v), (tx, tx_v),
        (sup, sup_v), (thr, thr_v), (sb, sb_v), (samples, s_v),
    ]
    copies = [
        pltpu.make_async_copy(src, dst, in_sem.at[i]) for i, (src, dst) in enumerate(loads)
    ]
    for copy in copies:
        copy.start()

    barrier = pltpu.get_barrier_semaphore()

    def greet(x, y):
        pl.semaphore_signal(barrier, inc=1, device_id={"gx": x, "gy": y}, device_id_type=MESH)

    @pl.loop(1, NX)
    def _(d):
        greet(lax.rem(gx + d, NX), gy)

    @pl.loop(1, NY)
    def _(d):
        greet(gx, lax.rem(gy + d, NY))

    @pl.loop(0, NX)
    def _(d):
        @pl.when(jnp.logical_not(jnp.logical_and(own, d == gx)))
        def _():
            greet(d, owner)

    @pl.loop(0, NX)
    def _(d):
        x, y = gy * 2 + lax.rem(d, 2), d // 2

        @pl.when(jnp.logical_not(jnp.logical_and(own, x == gx) & (y == gy)))
        def _():
            greet(x, y)

    copies[1].wait()
    copies[0].wait()
    e = eb_v[...]
    ea[...] = jnp.concatenate([e, jnp.zeros_like(e)], axis=0)
    ez[...] = jnp.concatenate([jnp.zeros_like(e), e], axis=0)
    for b in range(0, NY, 4):
        rows_a = jnp.concatenate([m_v[pl.ds(128 * j, 64), :] for j in range(b, b + 4)], axis=0)
        rows_b = jnp.concatenate([m_v[pl.ds(128 * j + 64, 64), :] for j in range(b, b + 4)], axis=0)
        packed = dot(rows_a, ea[...], LAST) + dot(rows_b, ez[...], LAST)
        s1[b : b + 4] = packed.astype(BF).reshape(4, 64, 128)

    pl.semaphore_wait(barrier, jnp.where(own, 52, 54))

    def along_y(i, src, dst):
        @pl.loop(1, NY)
        def _(d):
            j = lax.rem(gy + d, NY)
            pltpu.make_async_remote_copy(
                src_ref=src.at[j], dst_ref=dst.at[gy], send_sem=send_sem.at[i],
                recv_sem=recv_sem.at[i], device_id={"gy": j}, device_id_type=MESH,
            ).start()

        pltpu.make_async_copy(src.at[gy], dst.at[gy], recv_sem.at[i]).start()

    def along_x(i, src, dst):
        @pl.loop(1, NX)
        def _(d):
            j = lax.rem(gx + d, NX)
            pltpu.make_async_remote_copy(
                src_ref=src.at[j], dst_ref=dst.at[gx], send_sem=send_sem.at[i],
                recv_sem=recv_sem.at[i], device_id={"gx": j}, device_id_type=MESH,
            ).start()

        pltpu.make_async_copy(src.at[gx], dst.at[gx], recv_sem.at[i]).start()

    def across(i, src, dst, slot, target):
        @pl.loop(0, NX)
        def _(d):
            j = lax.rem(gx + d, NX)
            x, y = target(j)
            mine = jnp.logical_and(x == gx, y == gy)

            @pl.when(jnp.logical_not(mine))
            def _():
                pltpu.make_async_remote_copy(
                    src_ref=src.at[j], dst_ref=dst.at[slot], send_sem=send_sem.at[i],
                    recv_sem=recv_sem.at[i], device_id={"gx": x, "gy": y}, device_id_type=MESH,
                ).start()

            @pl.when(mine)
            def _():
                pltpu.make_async_copy(src.at[j], dst.at[slot], recv_sem.at[i]).start()

    def arrive(i, dst):
        pltpu.make_async_copy(dst, dst, recv_sem.at[i]).wait()

    along_y(0, s1, r1)

    copies[2].wait()
    for p in range(NY // 2):
        by[:, 128 * p : 128 * p + 128] = jnp.concatenate([ty_v[2 * p], ty_v[2 * p + 1]], axis=1)
    arrive(0, r1)
    lows, highs = zip(*[halves(r1[2 * p], r1[2 * p + 1]) for p in range(NY // 2)])
    rows = jnp.concatenate(
        [jnp.concatenate(lows, axis=1), jnp.concatenate(highs, axis=1)], axis=0
    )
    mixed = dot(rows, by[...], LAST).astype(BF)
    for p in range(NY // 2):
        part = mixed[:, 128 * p : 128 * p + 128]
        for h in range(2):
            even, odd = halves(part[64 * h : 64 * h + 32], part[64 * h + 32 : 64 * h + 64])
            s2[4 * p + h] = even
            s2[4 * p + 2 + h] = odd
    along_x(1, s2, r2)

    copies[3].wait()
    for p in range(NX // 2):
        bx[:, 128 * p : 128 * p + 128] = jnp.concatenate([tx_v[2 * p], tx_v[2 * p + 1]], axis=1)

    def gathered(r):
        lows, highs = zip(*[halves(r[2 * p], r[2 * p + 1]) for p in range(NX // 2)])
        return jnp.concatenate(
            [jnp.concatenate(lows, axis=1), jnp.concatenate(highs, axis=1)], axis=0
        )

    def spread(mixed, s):
        for p in range(NX // 2):
            part = mixed[:, 128 * p : 128 * p + 128]
            s[2 * p], s[2 * p + 1] = halves(part[:32], part[32:])

    arrive(1, r2)
    spread(dot(gathered(r2), bx[...], LAST).astype(BF), s3)
    across(2, s3, r3, gy * 2 + half, lambda j: (j, owner))

    copies[4].wait()
    copies[5].wait()
    copies[6].wait()
    base = sb_v[...]
    sl[...] = jnp.concatenate([base, jnp.zeros_like(base)], axis=0)
    sh[...] = jnp.concatenate([jnp.zeros_like(base), base], axis=0)
    supt[...] = jnp.transpose(sup_v[...])
    words = lax.broadcasted_iota(jnp.int32, (16, 128), 0)

    def gather_bits(i, acc):
        tile = supt[pl.ds(pl.multiple_of(i * 8, 8), 8), :]
        word = lax.shift_right_logical(tile, 5)
        bit = lax.shift_left(jnp.ones_like(tile), tile & 31)
        for n in range(8):
            hit = words == word[n : n + 1, :]
            acc = acc | jnp.where(hit, bit[n : n + 1, :], 0)
        return acc

    bits[...] = lax.fori_loop(0, 32, gather_bits, jnp.zeros((16, 128), jnp.int32))
    place = lax.broadcasted_iota(jnp.int32, (32, 128), 0)
    diagonal = lax.broadcasted_iota(jnp.int32, (16, 16), 0) == lax.broadcasted_iota(
        jnp.int32, (16, 16), 1
    )
    columns = [
        jnp.sum(jnp.where(diagonal, thr_v[l : l + 1, :], 0.0), axis=1, keepdims=True)
        for l in range(8)
    ]
    column = jnp.concatenate(columns, axis=0)
    for c in range(4):
        stacked = jnp.concatenate(
            [lax.shift_right_logical(jnp.broadcast_to(bits[4 * c + w : 4 * c + w + 1, :], (32, 128)), place) & 1
             for w in range(4)],
            axis=0,
        )
        kept = jnp.transpose(stacked.astype(F32))
        teff[:, 128 * c : 128 * c + 128] = jnp.where(kept > 0.0, column, jnp.inf)
    copies[7].wait()

    arrive(2, r3)
    for c in range(4):
        low = r3[4 * c : 4 * c + 4].reshape(128, 128)
        total = None
        for w, basis in enumerate((sl, sh)):
            predicted = dot(low, basis[...])
            held = s_v[4 * c : 4 * c + 4, w].reshape(128, 512).astype(F32)
            res = (held - predicted).astype(BF)
            res_v[4 * c : 4 * c + 4, w] = res.reshape(4, 32, 512)
            back = dot(res, basis[...], LAST)
            total = back if total is None else total + back
        s4[4 * c : 4 * c + 4] = total.astype(BF).reshape(4, 32, 128)
    across(3, s4, r4, gx, lambda j: (gy * 2 + lax.rem(j, 2), j // 2))
    res_out = pltpu.make_async_copy(res_v, out_res, out_sem.at[0])
    res_out.start()

    arrive(3, r4)
    spread(dot(gathered(r4), bx[...]).astype(BF), s5)
    along_x(4, s5, r5)

    arrive(4, r5)
    blocks = []
    for h in range(2):
        lows, highs = zip(*[halves(r5[4 * p + h], r5[4 * p + 2 + h]) for p in range(NY // 2)])
        blocks += [jnp.concatenate(lows, axis=1), jnp.concatenate(highs, axis=1)]
    mixed = dot(jnp.concatenate(blocks, axis=0), by[...]).astype(BF)
    for p in range(NY // 2):
        part = mixed[:, 128 * p : 128 * p + 128]
        s6[2 * p], s6[2 * p + 1] = halves(part[:64], part[64:])
    along_y(5, s6, r6)

    arrive(5, r6)
    for b in range(NY):
        back_top = r6[b]
        for w, basis in enumerate((ea, ez)):
            v = m_v[pl.ds(128 * b + 64 * w, 64), :].astype(F32) + dot(back_top, basis[...])
            t = teff[64 * w : 64 * w + 64, :]
            om_v[pl.ds(128 * b + 64 * w, 64), :] = v - jnp.minimum(jnp.maximum(v, -t), t)
    model_out = pltpu.make_async_copy(om_v, out_model, out_sem.at[1])
    model_out.start()

    for i, (src, per) in enumerate(((s1, 7), (s2, 15), (s3, 15), (s4, 15), (s5, 15), (s6, 7))):
        sent = src.at[pl.ds(0, per)]
        pltpu.make_async_copy(sent, sent, send_sem.at[i]).wait()

    @pl.when(jnp.logical_not(own))
    def _():
        for i, src in ((2, s3), (3, s4)):
            pltpu.make_async_copy(src.at[0], src.at[0], send_sem.at[i]).wait()

    res_out.wait()
    model_out.wait()


def on_device(
    samples, model_prev, threshold, support, sample_basis, eval_basis, transfer_x, transfer_y
):
    hbm = pl.BlockSpec(memory_space=pltpu.HBM)
    wide = pltpu.VMEM((8, 64, 128), BF)
    thin = pltpu.VMEM((16, 32, 128), BF)
    model_next, residual = pl.pallas_call(
        kernel,
        out_shape=(
            jax.ShapeDtypeStruct((1024, 512), F32),
            jax.ShapeDtypeStruct((16, 2, 32, 512), BF),
        ),
        in_specs=[hbm] * 8,
        out_specs=(hbm, hbm),
        scratch_shapes=[
            pltpu.VMEM((1024, 512), BF),
            pltpu.VMEM((16, 2, 32, 512), BF),
            pltpu.VMEM((16, 1024, 64), BF),
            pltpu.VMEM((8, 512, 64), BF),
            pltpu.VMEM((1024, 1024), BF),
            pltpu.VMEM((512, 512), BF),
            pltpu.VMEM((64, 512), BF),
            pltpu.VMEM((64, 512), BF),
            pltpu.VMEM((128, 512), BF),
            pltpu.VMEM((128, 512), BF),
            pltpu.VMEM((128, 512), BF),
            pltpu.VMEM((128, 512), BF),
            pltpu.VMEM((128, 256), jnp.int32),
            pltpu.VMEM((256, 128), jnp.int32),
            pltpu.VMEM((16, 128), jnp.int32),
            pltpu.VMEM((8, 16), F32),
            pltpu.VMEM((128, 512), F32),
            pltpu.VMEM((16, 2, 32, 512), BF),
            pltpu.VMEM((1024, 512), F32),
            wide, thin, thin, thin, thin, wide,
            wide, thin, thin, thin, thin, wide,
            pltpu.SemaphoreType.DMA((8,)),
            pltpu.SemaphoreType.DMA((2,)),
            pltpu.SemaphoreType.DMA((6,)),
            pltpu.SemaphoreType.DMA((6,)),
        ],
        compiler_params=pltpu.CompilerParams(
            collective_id=0, has_side_effects=True, vmem_limit_bytes=58 * 2**20
        ),
    )(
        samples.reshape(16, 2, 32, 512),
        model_prev.reshape(1024, 512),
        threshold,
        support.reshape(128, 256),
        sample_basis.T,
        eval_basis,
        transfer_x.reshape(16, 1024, 64),
        transfer_y.reshape(8, 512, 64),
    )
    return model_next.reshape(8, 8, 16, 512), residual.reshape(8, 8, 16, 512)


def solution(mesh):
    return jax.shard_map(
        on_device,
        mesh=mesh,
        in_specs=(
            P("ga", "gx", "gy", None),
            P("ga", "gx", "gy", None),
            P("gx", "gy"),
            P("gx", "gy", None),
            P(),
            P(),
            P(),
            P(),
        ),
        out_specs=(P("ga", "gx", "gy", None), P("ga", "gx", "gy", None)),
        check_vma=False,
    )
```

time: 348 us -> 67 us (0.19)
  waiting for transfers between devices: 264 us -> 0 us
  Pallas kernels: 0 us -> 61.6 us
  local copies, waits for them, and re-layouts: 38.5 us -> 4.28 us
  matrix products: 16.1 us -> 0 us
  other arithmetic: 14.5 us -> 0 us
  between operations: 13.9 us -> 0.65 us
    reduce_scatter x4 -> x0, waiting for transfers between devices: 263 us -> none  [the longest x2 149 us: level_y(): lax.psum_scatter(term(jnp.int32(0), lax.axis_size('gy') * row_count), 'gy...]
    pallas_call x0 -> x1, Pallas kernels: none -> 61.6 us  [on_device(): pl.pallas_call(kernel, out_shape=(jax.ShapeDtypeStruct((1024, 512), F32),...]
    dot_general x6 -> x0, matrix products: 16.1 us -> none  [the longest x4 13.3 us: term(): jnp.einsum('glmk,akq->aglmq', coeffs, column, preferred_element_type=jnp....]
    convert_element_type x6 -> x0, local copies, waits for them, and re-layouts: 15.6 us -> none  [the longest x2 13 us: level_x(): term(jnp.int32(0), row_count * lax.axis_size('gx')).astype(jnp.bfloat16)]
    reduce_or x1 -> x0, other arithmetic: 12.5 us -> none  [on_device(): jnp.any(support[:, :, :, None] == sample_slots[None, None, None, :], axis=2)]
    transpose x2 -> x0, local copies, waits for them, and re-layouts: 10 us -> none  [term(): jnp.einsum('glmk,akq->aglmq', coeffs, column, preferred_element_type=jnp....]
    reshape x2 -> x0, local copies, waits for them, and re-layouts: 9.54 us -> none  [term(): produced.reshape(box_count * row_count, coeffs.shape[2] * column.shape[-1])]
  transfers between devices with their start and end apart: 4 -> 0, of which waited for: 4 -> 0; matrix products, arithmetic and copies ran while one was open for 4% -> 0% of each run, Pallas kernels for 0% -> 0%
where the time goes in v1:
time: 67 us; the launch traced here: 66.6 us
  Pallas kernels  61.6 us (92%)
  local copies, waits for them, and re-layouts  4.28 us (6%)
    pallas_call x1, Pallas kernels, on_device(): pl.pallas_call(kernel, out_shape=(jax.ShapeDtypeStruct((1024, 512), F32),...  61.6 us
    unnamed x4, local copies, waits for them, and re-layouts  4.28 us

profile of v1, /device:TPU:1, one launch (start us, length us, event | category | flops | bytes accessed | tf_op | source)
XLA Modules:
  0.0 66.6 jit_solution(5203820187354426621)
XLA Ops:
  0.6 61.6 %shard_map.95 = (f32[1024,512]{1,0:T(8,128)}, bf16[16,2,32,512]{3,2,1,0:T(8,128)(2,1)}) custom-call(bf16[16,2,32,512]{3,2,1,0:T(8,128)(2,1)} %bitcast.10, bf16[1024,512]{1,0:T(8,128)(2,1)} %bitcast.11, f32[8,16]{1,0:T(8,128)} %thr.1, s32[128,256]{1,0:T(8,128)} %bitcast.14, bf16[64,512]{1,0:T(8,128)(2,1)} %bitcast.15, bf16[64,512]{1,0:T(8,128)(2,1)} %eb.1, ...), custom_call_target="tpu_custom_call" | custom-call | tf_op jit(solution)/shard_map/pallas_call | solution.py:270
  62.3 0.0 copy-start
  62.3 3.3 %copy.12 = f32[8,8,16,512]{3,2,1,0:T(8,128)} copy(f32[8,8,16,512]{3,2,1,0:T(8,128)} %bitcast.9) | data formatting | bytes 4194304
  65.6 0.0 copy-done
  65.6 1.0 %copy.13 = bf16[8,8,16,512]{3,2,1,0:T(8,128)(2,1)} copy(bf16[8,8,16,512]{3,2,1,0:T(8,128)(2,1)S(1)} %bitcast.13) | data formatting | bytes 2097152
Async XLA Ops:
  62.3 3.3 %copy-start = (bf16[16,2,32,512]{3,2,1,0:T(8,128)(2,1)S(1)}, bf16[16,2,32,512]{3,2,1,0:T(8,128)(2,1)}, u32[]{:S(2)}) copy-start(bf16[16,2,32,512]{3,2,1,0:T(8,128)(2,1)} %get-tuple-element.5) | copy-start | bytes 3145732

commit v2 on v0

v2 whole, which is shorter than its diff:
```python
import jax
import jax.numpy as jnp
from jax import lax
from jax.experimental import pallas as pl
from jax.experimental.pallas import tpu as pltpu
from jax.sharding import PartitionSpec as P

BF = jnp.bfloat16
F32 = jnp.float32
MESH = pl.DeviceIdType.MESH
NX, NY = 16, 8
N = NX * NY
LAST = (((1,), (1,)), ((), ()))
PLAIN = (((1,), (0,)), ((), ()))


def dot(a, b, dims=PLAIN):
    return lax.dot_general(a, b, dims, preferred_element_type=F32)


def kernel(
    samples, model, thr, sup, sb, eb, tx, ty,
    om_v, res_v,
    m_v, s_v, tx_v, ty_v, bx, by, sb_v, eb_v, e_lo, s_lo, e_hi, s_hi, gram, sup_v, supt, bits, thr_v, teff,
    top_out, top_in, smp_out, smp_in, low_out, low_home, back_out, back_home,
    in_sem, send_sem, recv_sem,
):
    gx, gy = lax.axis_index("gx"), lax.axis_index("gy")
    me = gx * NY + gy
    left = lax.broadcasted_iota(jnp.int32, (8, 128), 1) < 64
    straight = left == (lax.broadcasted_iota(jnp.int32, (8, 128), 0) < 4)

    def swap(u):
        return pltpu.roll(u, 64, 1)

    def turn(u):
        return jnp.where(straight, u, pltpu.roll(swap(u), 4, 0))

    loads = [
        (model, m_v), (eb, eb_v), (sb, sb_v), (samples, s_v),
        (ty, ty_v), (tx, tx_v), (sup, sup_v), (thr, thr_v),
    ]
    copies = [
        pltpu.make_async_copy(src, dst, in_sem.at[i]) for i, (src, dst) in enumerate(loads)
    ]
    for copy in copies[:4]:
        copy.start()

    def plane(i):
        away = (i + 1) // 2
        return lax.rem(gx // 2 + 4 + jnp.where(lax.rem(i, 2) == 0, away, 8 - away), 8)

    columns_y = [lax.rem(gy + d, NY) for d in (6, 2, 5, 3, 4, 7, 1)] + [gy]

    def each_partner(act):
        @pl.loop(0, NX - 1)
        def _(i):
            away = (i + 1) // 2
            x = lax.rem(gx + 8 + jnp.where(lax.rem(i, 2) == 0, away, NX - away), NX)
            for y in columns_y:
                act(x, y)

        for y in columns_y[:-1]:
            act(gx, y)

    barrier = pltpu.get_barrier_semaphore()

    each_partner(
        lambda x, y: pl.semaphore_signal(
            barrier, inc=1, device_id={"gx": x, "gy": y}, device_id_type=MESH
        )
    )

    copies[1].wait()
    e = eb_v[...]
    zero = jnp.zeros_like(e)
    e_lo[...] = jnp.concatenate([e, zero], axis=0)
    e_hi[...] = jnp.concatenate([zero, e], axis=0)
    copies[2].wait()
    base = sb_v[...]
    s_lo[...] = jnp.concatenate([base, zero], axis=0)
    s_hi[...] = jnp.concatenate([zero, base], axis=0)
    copies[0].wait()
    for copy in copies[4:]:
        copy.start()
    top_out[...] = (dot(m_v[:512], e_lo[...], LAST) + dot(m_v[512:], e_hi[...], LAST)).astype(BF)

    pl.semaphore_wait(barrier, N - 1)

    def slot(i):
        return pl.ds(pl.multiple_of(i * 4, 4), 4)

    def along(x, y):
        return x * NY + y

    def crossed(x, y):
        return y * NX + x

    def exchange(i, src, at, dst, here, arrived):
        def send(x, y):
            pltpu.make_async_remote_copy(
                src_ref=src.at[slot(at(x, y))], dst_ref=dst.at[slot(here)],
                send_sem=send_sem.at[i], recv_sem=arrived,
                device_id={"gx": x, "gy": y}, device_id_type=MESH,
            ).start()

        each_partner(send)
        pltpu.make_async_copy(src.at[slot(at(gx, gy))], dst.at[slot(here)], arrived).start()

    def arrive(dst, arrived):
        pltpu.make_async_copy(dst, dst, arrived).wait()

    exchange(0, top_out, along, top_in, crossed(gx, gy), recv_sem.at[8])

    copies[3].wait()
    smp_out[...] = (dot(s_v[:512], s_lo[...], LAST) + dot(s_v[512:], s_hi[...], LAST)).astype(BF)
    exchange(1, smp_out, along, smp_in, me, recv_sem.at[9])

    copies[4].wait()
    for p in range(NY // 2):
        by[:, 128 * p : 128 * p + 128] = jnp.concatenate([ty_v[2 * p], ty_v[2 * p + 1]], axis=1)
    copies[5].wait()
    for p in range(NX // 2):
        bx[:, 128 * p : 128 * p + 128] = jnp.concatenate([tx_v[2 * p], tx_v[2 * p + 1]], axis=1)

    block = dot(s_lo[...], s_lo[...], LAST) + dot(s_hi[...], s_hi[...], LAST)
    major = block.astype(BF)
    gram[:128] = major
    gram[128:] = (block - major.astype(F32)).astype(BF)

    copies[6].wait()
    copies[7].wait()
    supt[...] = jnp.transpose(sup_v[...])
    words = lax.broadcasted_iota(jnp.int32, (16, 128), 0)

    def gather_bits(i, acc):
        tile = supt[pl.ds(pl.multiple_of(i * 8, 8), 8), :]
        word = lax.shift_right_logical(tile, 5)
        bit = lax.shift_left(jnp.ones_like(tile), tile & 31)
        for n in range(8):
            hit = words == word[n : n + 1, :]
            acc = acc | jnp.where(hit, bit[n : n + 1, :], 0)
        return acc

    bits[...] = lax.fori_loop(0, 32, gather_bits, jnp.zeros((16, 128), jnp.int32))
    place = lax.broadcasted_iota(jnp.int32, (32, 128), 0)
    diagonal = lax.broadcasted_iota(jnp.int32, (16, 16), 0) == lax.broadcasted_iota(
        jnp.int32, (16, 16), 1
    )
    columns = [
        jnp.sum(jnp.where(diagonal, thr_v[l : l + 1, :], 0.0), axis=1, keepdims=True)
        for l in range(8)
    ]
    column = jnp.concatenate(columns, axis=0)
    for c in range(4):
        stacked = jnp.concatenate(
            [lax.shift_right_logical(jnp.broadcast_to(bits[4 * c + w : 4 * c + w + 1, :], (32, 128)), place) & 1
             for w in range(4)],
            axis=0,
        )
        kept = jnp.transpose(stacked.astype(F32))
        teff[:, 128 * c : 128 * c + 128] = jnp.where(kept > 0.0, column, jnp.inf)

    def tile(ref, i):
        return ref[pl.ds(4 * i, 8), :].astype(F32)

    def assembled(parts):
        return jnp.concatenate([jnp.concatenate(row, axis=1) for row in parts], axis=0)

    def paired(ref, i, k):
        u, v = tile(ref, i), tile(ref, k)
        return jnp.where(left, u, swap(v)), jnp.where(left, swap(u), v)

    def part(u, i, k):
        return u[8 * i : 8 * i + 8, 128 * k : 128 * k + 128]

    HX, HY = NX // 2, NY // 2
    arrive(top_in, recv_sem.at[8])
    parts = [[None] * HY for _ in range(NX)]
    for q in range(HX):
        for p in range(HY):
            parts[q][p], parts[HX + q][p] = paired(
                top_in, crossed(2 * q, 2 * p), crossed(2 * q, 2 * p + 1)
            )
    middle = dot(assembled(parts).astype(BF), by[...], LAST)
    low = dot(
        assembled(
            [[turn(part(middle, HX * w + q, p)) for q in range(HX)] for w in range(2) for p in range(HY)]
        ).astype(BF),
        bx[...],
        LAST,
    )
    for q in range(HX):
        for p in range(HY):
            u, v = part(low, p, q), part(low, HY + p, q)
            low_out[pl.ds(4 * along(2 * q, 2 * p), 8), :] = jnp.where(left, u, swap(v)).astype(BF)
            low_out[pl.ds(4 * along(2 * q + 1, 2 * p), 8), :] = jnp.where(left, swap(u), v).astype(BF)
    exchange(2, low_out, along, low_home, me, recv_sem.at[10])

    low_bf = low.astype(BF)
    stacked = jnp.concatenate([low_bf[:, 128 * q : 128 * q + 128] for q in range(HX)], axis=0)
    taken = dot(stacked, gram[:128]) + dot(stacked, gram[128:])
    arrive(smp_in, recv_sem.at[9])
    parts = [[None] * HX for _ in range(NY)]
    for q in range(HX):
        for p in range(HY):
            u, v = paired(smp_in, along(2 * q, 2 * p), along(2 * q + 1, 2 * p))
            parts[p][q] = u - part(taken, NY * q + p, 0)
            parts[HY + p][q] = v - part(taken, NY * q + HY + p, 0)
    back_mid = dot(assembled(parts).astype(BF), bx[...])
    back_top = dot(
        assembled(
            [[turn(part(back_mid, HY * w + p, q)) for p in range(HY)] for w in range(2) for q in range(HX)]
        ).astype(BF),
        by[...],
    )
    for q in range(HX):
        for p in range(HY):
            u, v = part(back_top, q, p), part(back_top, HX + q, p)
            back_out[pl.ds(4 * crossed(2 * q, 2 * p), 8), :] = jnp.where(left, u, swap(v)).astype(BF)
            back_out[pl.ds(4 * crossed(2 * q, 2 * p + 1), 8), :] = jnp.where(left, swap(u), v).astype(BF)
    exchange(3, back_out, crossed, back_home, me, recv_sem.at[gx // 2])

    arrive(low_home, recv_sem.at[10])
    for w, basis in enumerate((s_lo, s_hi)):
        for b in range(4):
            block = pl.ds(512 * w + 128 * b, 128)
            predicted = dot(low_home[pl.ds(128 * b, 128), :], basis[...])
            res_v[block, :] = (s_v[block, :].astype(F32) - predicted).astype(BF)

    @pl.loop(0, 8)
    def _(i):
        z = plane(i)
        rows = pl.ds(pl.multiple_of(64 * z, 64), 64)
        arrive(back_home.at[rows], recv_sem.at[z])
        home = back_home[rows, :]
        t = teff[pl.ds(pl.multiple_of(64 * lax.rem(z, 2), 64), 64), :]
        for w, basis in enumerate((e_lo, e_hi)):
            block = pl.ds(pl.multiple_of(512 * w + 64 * z, 64), 64)
            v = m_v[block, :].astype(F32) + dot(home, basis[...])
            om_v[block, :] = v - jnp.minimum(jnp.maximum(v, -t), t)

    for i, src in enumerate((top_out, smp_out, low_out, back_out)):
        sent = src.at[pl.ds(0, 4 * (N - 1))]
        pltpu.make_async_copy(sent, sent, send_sem.at[i]).wait()


def on_device(
    samples, model_prev, threshold, support, sample_basis, eval_basis, transfer_x, transfer_y
):
    hbm = pl.BlockSpec(memory_space=pltpu.HBM)
    traffic = pltpu.VMEM((4 * N, 128), BF)
    model_next, residual = pl.pallas_call(
        kernel,
        out_shape=(
            jax.ShapeDtypeStruct((1024, 512), F32),
            jax.ShapeDtypeStruct((1024, 512), BF),
        ),
        in_specs=[hbm] * 8,
        out_specs=(pl.BlockSpec(memory_space=pltpu.VMEM),) * 2,
        scratch_shapes=[
            pltpu.VMEM((1024, 512), BF),
            pltpu.VMEM((1024, 512), BF),
            pltpu.VMEM((16, 1024, 64), BF),
            pltpu.VMEM((8, 512, 64), BF),
            pltpu.VMEM((1024, 1024), BF),
            pltpu.VMEM((512, 512), BF),
            pltpu.VMEM((64, 512), BF),
            pltpu.VMEM((64, 512), BF),
            pltpu.VMEM((128, 512), BF),
            pltpu.VMEM((128, 512), BF),
            pltpu.VMEM((128, 512), BF),
            pltpu.VMEM((128, 512), BF),
            pltpu.VMEM((256, 128), BF),
            pltpu.VMEM((128, 256), jnp.int32),
            pltpu.VMEM((256, 128), jnp.int32),
            pltpu.VMEM((16, 128), jnp.int32),
            pltpu.VMEM((8, 16), F32),
            pltpu.VMEM((128, 512), F32),
            traffic, traffic, traffic, traffic, traffic, traffic, traffic, traffic,
            pltpu.SemaphoreType.DMA((8,)),
            pltpu.SemaphoreType.DMA((4,)),
            pltpu.SemaphoreType.DMA((11,)),
        ],
        compiler_params=pltpu.CompilerParams(
            collective_id=0, has_side_effects=True, vmem_limit_bytes=30 * 2**20
        ),
    )(
        *[pltpu.with_memory_space_constraint(v, pltpu.HBM) for v in (
        samples.reshape(1024, 512),
        model_prev.reshape(1024, 512),
        threshold,
        support.reshape(128, 256),
        sample_basis.T,
        eval_basis,
        transfer_x.reshape(16, 1024, 64),
        transfer_y.reshape(8, 512, 64),
    )])
    return model_next.reshape(8, 8, 16, 512), residual.reshape(8, 8, 16, 512)


def solution(mesh):
    return jax.shard_map(
        on_device,
        mesh=mesh,
        in_specs=(
            P("ga", "gx", "gy", None),
            P("ga", "gx", "gy", None),
            P("gx", "gy"),
            P("gx", "gy", None),
            P(),
            P(),
            P(),
            P(),
        ),
        out_specs=(P("ga", "gx", "gy", None), P("ga", "gx", "gy", None)),
        check_vma=False,
    )
```

time: 348 us -> 38.4 us (0.11)
  waiting for transfers between devices: 264 us -> 0 us
  local copies, waits for them, and re-layouts: 38.5 us -> 2.29 us
  Pallas kernels: 0 us -> 35.4 us
  matrix products: 16.1 us -> 0 us
  other arithmetic: 14.5 us -> 0 us
  between operations: 13.9 us -> 0.64 us
    reduce_scatter x4 -> x0, waiting for transfers between devices: 263 us -> none  [the longest x2 149 us: level_y(): lax.psum_scatter(term(jnp.int32(0), lax.axis_size('gy') * row_count), 'gy...]
    pallas_call x0 -> x1, Pallas kernels: none -> 35.4 us  [on_device(): pl.pallas_call(kernel, out_shape=(jax.ShapeDtypeStruct((1024, 512), F32),...]
    dot_general x6 -> x0, matrix products: 16.1 us -> none  [the longest x4 13.3 us: term(): jnp.einsum('glmk,akq->aglmq', coeffs, column, preferred_element_type=jnp....]
    convert_element_type x6 -> x0, local copies, waits for them, and re-layouts: 15.6 us -> none  [the longest x2 13 us: level_x(): term(jnp.int32(0), row_count * lax.axis_size('gx')).astype(jnp.bfloat16)]
    reduce_or x1 -> x0, other arithmetic: 12.5 us -> none  [on_device(): jnp.any(support[:, :, :, None] == sample_slots[None, None, None, :], axis=2)]
    transpose x2 -> x0, local copies, waits for them, and re-layouts: 10 us -> none  [term(): jnp.einsum('glmk,akq->aglmq', coeffs, column, preferred_element_type=jnp....]
    reshape x2 -> x0, local copies, waits for them, and re-layouts: 9.54 us -> none  [term(): produced.reshape(box_count * row_count, coeffs.shape[2] * column.shape[-1])]
  transfers between devices with their start and end apart: 4 -> 0, of which waited for: 4 -> 0; matrix products, arithmetic and copies ran while one was open for 4% -> 0% of each run, Pallas kernels for 0% -> 0%
where the time goes in v2:
time: 38.4 us; the launch traced here: 38.3 us
  Pallas kernels  35.4 us (92%)
  local copies, waits for them, and re-layouts  2.29 us (6%)
  between operations  0.64 us (2%)
    pallas_call x1, Pallas kernels, on_device(): pl.pallas_call(kernel, out_shape=(jax.ShapeDtypeStruct((1024, 512), F32),...  35.4 us
    unnamed x2, local copies, waits for them, and re-layouts  2.29 us

profile of v2, /device:TPU:1, one launch (start us, length us, event | category | flops | bytes accessed | tf_op | source)
XLA Modules:
  0.0 38.3 jit_solution(12728641720709513548)
XLA Ops:
  0.6 35.4 %shard_map.95 = (f32[1024,512]{1,0:T(8,128)S(1)}, bf16[1024,512]{1,0:T(8,128)(2,1)S(1)}) custom-call(bf16[1024,512]{1,0:T(8,128)(2,1)} %bitcast.11, bf16[1024,512]{1,0:T(8,128)(2,1)} %bitcast.12, f32[8,16]{1,0:T(8,128)} %thr.1, s32[128,256]{1,0:T(8,128)} %bitcast.14, bf16[64,512]{1,0:T(8,128)(2,1)} %bitcast.15, bf16[64,512]{1,0:T(8,128)(2,1)} %eb.1, ...), custom_call_target="tpu_custom_call" | custom-call | tf_op jit(solution)/shard_map/pallas_call | solution.py:253
  36.0 1.3 %copy.12 = f32[8,8,16,512]{3,2,1,0:T(8,128)} copy(f32[8,8,16,512]{3,2,1,0:T(8,128)S(1)} %bitcast.8) | data formatting | bytes 4194304
  37.3 1.0 %copy.13 = bf16[8,8,16,512]{3,2,1,0:T(8,128)(2,1)} copy(bf16[8,8,16,512]{3,2,1,0:T(8,128)(2,1)S(1)} %bitcast.9) | data formatting | bytes 2097152

commit v3 on v2

--- a/solution.py
+++ b/solution.py
@@ -43,8 +43,6 @@
     copies = [
         pltpu.make_async_copy(src, dst, in_sem.at[i]) for i, (src, dst) in enumerate(loads)
     ]
-    for copy in copies[:4]:
-        copy.start()
 
     def plane(i):
         away = (i + 1) // 2
@@ -70,6 +68,8 @@
             barrier, inc=1, device_id={"gx": x, "gy": y}, device_id_type=MESH
         )
     )
+    for copy in copies:
+        copy.start()
 
     copies[1].wait()
     e = eb_v[...]
@@ -81,8 +81,6 @@
     s_lo[...] = jnp.concatenate([base, zero], axis=0)
     s_hi[...] = jnp.concatenate([zero, base], axis=0)
     copies[0].wait()
-    for copy in copies[4:]:
-        copy.start()
     top_out[...] = (dot(m_v[:512], e_lo[...], LAST) + dot(m_v[512:], e_hi[...], LAST)).astype(BF)
 
     pl.semaphore_wait(barrier, N - 1)
@@ -116,50 +114,17 @@
     smp_out[...] = (dot(s_v[:512], s_lo[...], LAST) + dot(s_v[512:], s_hi[...], LAST)).astype(BF)
     exchange(1, smp_out, along, smp_in, me, recv_sem.at[9])
 
+    block = dot(s_lo[...], s_lo[...], LAST) + dot(s_hi[...], s_hi[...], LAST)
+    major = block.astype(BF)
+    gram[:128] = major
+    gram[128:] = (block - major.astype(F32)).astype(BF)
+
     copies[4].wait()
     for p in range(NY // 2):
         by[:, 128 * p : 128 * p + 128] = jnp.concatenate([ty_v[2 * p], ty_v[2 * p + 1]], axis=1)
     copies[5].wait()
     for p in range(NX // 2):
         bx[:, 128 * p : 128 * p + 128] = jnp.concatenate([tx_v[2 * p], tx_v[2 * p + 1]], axis=1)
-
-    block = dot(s_lo[...], s_lo[...], LAST) + dot(s_hi[...], s_hi[...], LAST)
-    major = block.astype(BF)
-    gram[:128] = major
-    gram[128:] = (block - major.astype(F32)).astype(BF)
-
-    copies[6].wait()
-    copies[7].wait()
-    supt[...] = jnp.transpose(sup_v[...])
-    words = lax.broadcasted_iota(jnp.int32, (16, 128), 0)
-
-    def gather_bits(i, acc):
-        tile = supt[pl.ds(pl.multiple_of(i * 8, 8), 8), :]
-        word = lax.shift_right_logical(tile, 5)
-        bit = lax.shift_left(jnp.ones_like(tile), tile & 31)
-        for n in range(8):
-            hit = words == word[n : n + 1, :]
-            acc = acc | jnp.where(hit, bit[n : n + 1, :], 0)
-        return acc
-
-    bits[...] = lax.fori_loop(0, 32, gather_bits, jnp.zeros((16, 128), jnp.int32))
-    place = lax.broadcasted_iota(jnp.int32, (32, 128), 0)
-    diagonal = lax.broadcasted_iota(jnp.int32, (16, 16), 0) == lax.broadcasted_iota(
-        jnp.int32, (16, 16), 1
-    )
-    columns = [
-        jnp.sum(jnp.where(diagonal, thr_v[l : l + 1, :], 0.0), axis=1, keepdims=True)
-        for l in range(8)
-    ]
-    column = jnp.concatenate(columns, axis=0)
-    for c in range(4):
-        stacked = jnp.concatenate(
-            [lax.shift_right_logical(jnp.broadcast_to(bits[4 * c + w : 4 * c + w + 1, :], (32, 128)), place) & 1
-             for w in range(4)],
-            axis=0,
-        )
-        kept = jnp.transpose(stacked.astype(F32))
-        teff[:, 128 * c : 128 * c + 128] = jnp.where(kept > 0.0, column, jnp.inf)
 
     def tile(ref, i):
         return ref[pl.ds(4 * i, 8), :].astype(F32)
@@ -221,6 +186,39 @@
             back_out[pl.ds(4 * crossed(2 * q, 2 * p + 1), 8), :] = jnp.where(left, swap(u), v).astype(BF)
     exchange(3, back_out, crossed, back_home, me, recv_sem.at[gx // 2])
 
+    copies[6].wait()
+    copies[7].wait()
+    supt[...] = jnp.transpose(sup_v[...])
+    words = lax.broadcasted_iota(jnp.int32, (16, 128), 0)
+
+    def gather_bits(i, acc):
+        tile = supt[pl.ds(pl.multiple_of(i * 8, 8), 8), :]
+        word = lax.shift_right_logical(tile, 5)
+        bit = lax.shift_left(jnp.ones_like(tile), tile & 31)
+        for n in range(8):
+            hit = words == word[n : n + 1, :]
+            acc = acc | jnp.where(hit, bit[n : n + 1, :], 0)
+        return acc
+
+    bits[...] = lax.fori_loop(0, 32, gather_bits, jnp.zeros((16, 128), jnp.int32))
+    place = lax.broadcasted_iota(jnp.int32, (32, 128), 0)
+    diagonal = lax.broadcasted_iota(jnp.int32, (16, 16), 0) == lax.broadcasted_iota(
+        jnp.int32, (16, 16), 1
+    )
+    columns = [
+        jnp.sum(jnp.where(diagonal, thr_v[l : l + 1, :], 0.0), axis=1, keepdims=True)
+        for l in range(8)
+    ]
+    column = jnp.concatenate(columns, axis=0)
+    for c in range(4):
+        stacked = jnp.concatenate(
+            [lax.shift_right_logical(jnp.broadcast_to(bits[4 * c + w : 4 * c + w + 1, :], (32, 128)), place) & 1
+             for w in range(4)],
+            axis=0,
+        )
+        kept = jnp.transpose(stacked.astype(F32))
+        teff[:, 128 * c : 128 * c + 128] = jnp.where(kept > 0.0, column, jnp.inf)
+
     arrive(low_home, recv_sem.at[10])
     for w, basis in enumerate((s_lo, s_hi)):
         for b in range(4):
@@ -243,6 +241,17 @@
     for i, src in enumerate((top_out, smp_out, low_out, back_out)):
         sent = src.at[pl.ds(0, 4 * (N - 1))]
         pltpu.make_async_copy(sent, sent, send_sem.at[i]).wait()
+
+
+def deliver(model_v, residual_v, model_next, residual, sem):
+    copies = [
+        pltpu.make_async_copy(model_v, model_next, sem.at[0]),
+        pltpu.make_async_copy(residual_v, residual, sem.at[1]),
+    ]
+    for copy in copies:
+        copy.start()
+    for copy in copies:
+        copy.wait()
 
 
 def on_device(
@@ -296,6 +305,18 @@
         transfer_x.reshape(16, 1024, 64),
         transfer_y.reshape(8, 512, 64),
     )])
+    vmem = pl.BlockSpec(memory_space=pltpu.VMEM)
+    model_next, residual = pl.pallas_call(
+        deliver,
+        out_shape=(
+            jax.ShapeDtypeStruct((1024, 512), F32),
+            jax.ShapeDtypeStruct((1024, 512), BF),
+        ),
+        in_specs=[vmem, vmem],
+        out_specs=(hbm, hbm),
+        scratch_shapes=[pltpu.SemaphoreType.DMA((2,))],
+        compiler_params=pltpu.CompilerParams(vmem_limit_bytes=2 * 2**20),
+    )(model_next, residual)
     return model_next.reshape(8, 8, 16, 512), residual.reshape(8, 8, 16, 512)
 
 

time: 38.4 us -> 37.8 us (0.984)
  local copies, waits for them, and re-layouts: 2.29 us -> 0 us
  Pallas kernels: 35.4 us -> 37.1 us
    unnamed x2 -> x0, local copies, waits for them, and re-layouts: 2.29 us -> none
    pallas_call x0 -> x1, Pallas kernels: none -> 1.68 us  [on_device(): pl.pallas_call(deliver, out_shape=(jax.ShapeDtypeStruct((1024, 512), F32)...]
where the time goes in v3:
time: 37.8 us; the launch traced here: 37.7 us
  Pallas kernels  37.1 us (98%)
  between operations  0.64 us (2%)
    pallas_call x1, Pallas kernels, on_device(): pl.pallas_call(kernel, out_shape=(jax.ShapeDtypeStruct((1024, 512), F32),...  35.4 us
    pallas_call x1, Pallas kernels, on_device(): pl.pallas_call(deliver, out_shape=(jax.ShapeDtypeStruct((1024, 512), F32)...  1.68 us

profile of v3, /device:TPU:1, one launch (start us, length us, event | category | flops | bytes accessed | tf_op | source)
XLA Modules:
  0.0 37.7 jit_solution(2926882478459882527)
XLA Ops:
  0.6 35.4 %shard_map.95 = (f32[1024,512]{1,0:T(8,128)S(1)}, bf16[1024,512]{1,0:T(8,128)(2,1)S(1)}) custom-call(bf16[1024,512]{1,0:T(8,128)(2,1)} %bitcast.9, bf16[1024,512]{1,0:T(8,128)(2,1)} %bitcast.10, f32[8,16]{1,0:T(8,128)} %thr.1, s32[128,256]{1,0:T(8,128)} %bitcast.12, bf16[64,512]{1,0:T(8,128)(2,1)} %bitcast.13, bf16[64,512]{1,0:T(8,128)(2,1)} %eb.1, ...), custom_call_target="tpu_custom_call" | custom-call | tf_op jit(solution)/shard_map/pallas_call | solution.py:262
  36.0 1.7 %shard_map.96 = (f32[1024,512]{1,0:T(8,128)}, bf16[1024,512]{1,0:T(8,128)(2,1)}) custom-call(f32[1024,512]{1,0:T(8,128)S(1)} %get-tuple-element.6.model_v, bf16[1024,512]{1,0:T(8,128)(2,1)S(1)} %get-tuple-element.7.residual_v), custom_call_target="tpu_custom_call" | custom-call | tf_op jit(solution)/shard_map/pallas_call | solution.py:309

commit v4 on v3

--- a/solution.py
+++ b/solution.py
@@ -121,10 +121,21 @@
 
     copies[4].wait()
     for p in range(NY // 2):
-        by[:, 128 * p : 128 * p + 128] = jnp.concatenate([ty_v[2 * p], ty_v[2 * p + 1]], axis=1)
+        @pl.loop(0, 4)
+        def _(i):
+            rows = pl.ds(pl.multiple_of(128 * i, 128), 128)
+            by[rows, 128 * p : 128 * p + 128] = jnp.concatenate(
+                [ty_v[2 * p, rows, :], ty_v[2 * p + 1, rows, :]], axis=1
+            )
+
     copies[5].wait()
     for p in range(NX // 2):
-        bx[:, 128 * p : 128 * p + 128] = jnp.concatenate([tx_v[2 * p], tx_v[2 * p + 1]], axis=1)
+        @pl.loop(0, 8)
+        def _(i):
+            rows = pl.ds(pl.multiple_of(128 * i, 128), 128)
+            bx[rows, 128 * p : 128 * p + 128] = jnp.concatenate(
+                [tx_v[2 * p, rows, :], tx_v[2 * p + 1, rows, :]], axis=1
+            )
 
     def tile(ref, i):
         return ref[pl.ds(4 * i, 8), :].astype(F32)
@@ -220,23 +231,28 @@
         teff[:, 128 * c : 128 * c + 128] = jnp.where(kept > 0.0, column, jnp.inf)
 
     arrive(low_home, recv_sem.at[10])
-    for w, basis in enumerate((s_lo, s_hi)):
-        for b in range(4):
-            block = pl.ds(512 * w + 128 * b, 128)
-            predicted = dot(low_home[pl.ds(128 * b, 128), :], basis[...])
-            res_v[block, :] = (s_v[block, :].astype(F32) - predicted).astype(BF)
-
-    @pl.loop(0, 8)
+    @pl.loop(0, 4)
+    def _(b):
+        home = low_home[pl.ds(pl.multiple_of(128 * b, 128), 128), :]
+        for w, basis in enumerate((s_lo, s_hi)):
+            block = pl.ds(pl.multiple_of(512 * w + 128 * b, 128), 128)
+            res_v[block, :] = (s_v[block, :].astype(F32) - dot(home, basis[...])).astype(BF)
+
+    @pl.loop(0, 2)
     def _(i):
-        z = plane(i)
-        rows = pl.ds(pl.multiple_of(64 * z, 64), 64)
-        arrive(back_home.at[rows], recv_sem.at[z])
-        home = back_home[rows, :]
-        t = teff[pl.ds(pl.multiple_of(64 * lax.rem(z, 2), 64), 64), :]
+        zs = [plane(i * 4 + k) for k in range(4)]
+        for z in zs:
+            arrive(back_home.at[pl.ds(pl.multiple_of(64 * z, 64), 64)], recv_sem.at[z])
+        home = jnp.concatenate(
+            [back_home[pl.ds(pl.multiple_of(64 * z, 64), 64), :] for z in zs], axis=0
+        )
         for w, basis in enumerate((e_lo, e_hi)):
-            block = pl.ds(pl.multiple_of(512 * w + 64 * z, 64), 64)
-            v = m_v[block, :].astype(F32) + dot(home, basis[...])
-            om_v[block, :] = v - jnp.minimum(jnp.maximum(v, -t), t)
+            update = dot(home, basis[...])
+            for k, z in enumerate(zs):
+                block = pl.ds(pl.multiple_of(512 * w + 64 * z, 64), 64)
+                t = teff[pl.ds(pl.multiple_of(64 * lax.rem(z, 2), 64), 64), :]
+                v = m_v[block, :].astype(F32) + update[64 * k : 64 * k + 64]
+                om_v[block, :] = v - jnp.minimum(jnp.maximum(v, -t), t)
 
     for i, src in enumerate((top_out, smp_out, low_out, back_out)):
         sent = src.at[pl.ds(0, 4 * (N - 1))]

time: 37.8 us -> 37 us (0.979)
  Pallas kernels: 37.1 us -> 36.3 us
    pallas_call x1, Pallas kernels: 35.4 us -> 34.6 us  [on_device(): pl.pallas_call(kernel, out_shape=(jax.ShapeDtypeStruct((1024, 512), F32),...]
where the time goes in v4:
time: 37 us; the launch traced here: 36.9 us
  Pallas kernels  36.3 us (98%)
  between operations  0.64 us (2%)
    pallas_call x1, Pallas kernels, on_device(): pl.pallas_call(kernel, out_shape=(jax.ShapeDtypeStruct((1024, 512), F32),...  34.6 us
    pallas_call x1, Pallas kernels, on_device(): pl.pallas_call(deliver, out_shape=(jax.ShapeDtypeStruct((1024, 512), F32)...  1.68 us

profile of v4, /device:TPU:1, one launch (start us, length us, event | category | flops | bytes accessed | tf_op | source)
XLA Modules:
  0.0 36.9 jit_solution(16605388549661984106)
XLA Ops:
  0.6 34.6 %shard_map.95 = (f32[1024,512]{1,0:T(8,128)S(1)}, bf16[1024,512]{1,0:T(8,128)(2,1)S(1)}) custom-call(bf16[1024,512]{1,0:T(8,128)(2,1)} %bitcast.9, bf16[1024,512]{1,0:T(8,128)(2,1)} %bitcast.10, f32[8,16]{1,0:T(8,128)} %thr.1, s32[128,256]{1,0:T(8,128)} %bitcast.12, bf16[64,512]{1,0:T(8,128)(2,1)} %bitcast.13, bf16[64,512]{1,0:T(8,128)(2,1)} %eb.1, ...), custom_call_target="tpu_custom_call" | custom-call | tf_op jit(solution)/shard_map/pallas_call | solution.py:278
  35.2 1.7 %shard_map.96 = (f32[1024,512]{1,0:T(8,128)}, bf16[1024,512]{1,0:T(8,128)(2,1)}) custom-call(f32[1024,512]{1,0:T(8,128)S(1)} %get-tuple-element.6.model_v, bf16[1024,512]{1,0:T(8,128)(2,1)S(1)} %get-tuple-element.7.residual_v), custom_call_target="tpu_custom_call" | custom-call | tf_op jit(solution)/shard_map/pallas_call | solution.py:325

commit v5 on v4

--- a/solution.py
+++ b/solution.py
@@ -60,6 +60,19 @@
 
         for y in columns_y[:-1]:
             act(gx, y)
+
+    def each_below(ys, act):
+        @pl.loop(0, NX - 1)
+        def _(i):
+            away = (i + 1) // 2
+            x = lax.rem(gx + 8 + jnp.where(lax.rem(i, 2) == 0, away, NX - away), NX)
+            for y in ys:
+                act(x, y)
+
+        for y in ys:
+            @pl.when(y != gy)
+            def _():
+                act(gx, y)
 
     barrier = pltpu.get_barrier_semaphore()
 
@@ -184,18 +197,29 @@
             parts[p][q] = u - part(taken, NY * q + p, 0)
             parts[HY + p][q] = v - part(taken, NY * q + HY + p, 0)
     back_mid = dot(assembled(parts).astype(BF), bx[...])
-    back_top = dot(
-        assembled(
-            [[turn(part(back_mid, HY * w + p, q)) for p in range(HY)] for w in range(2) for q in range(HX)]
-        ).astype(BF),
-        by[...],
-    )
-    for q in range(HX):
-        for p in range(HY):
-            u, v = part(back_top, q, p), part(back_top, HX + q, p)
-            back_out[pl.ds(4 * crossed(2 * q, 2 * p), 8), :] = jnp.where(left, u, swap(v)).astype(BF)
-            back_out[pl.ds(4 * crossed(2 * q, 2 * p + 1), 8), :] = jnp.where(left, swap(u), v).astype(BF)
-    exchange(3, back_out, crossed, back_home, me, recv_sem.at[gx // 2])
+    turned = assembled(
+        [[turn(part(back_mid, HY * w + p, q)) for p in range(HY)] for w in range(2) for q in range(HX)]
+    ).astype(BF)
+
+    def send_back(x, y):
+        pltpu.make_async_remote_copy(
+            src_ref=back_out.at[slot(crossed(x, y))], dst_ref=back_home.at[slot(me)],
+            send_sem=send_sem.at[3], recv_sem=recv_sem.at[gx // 2],
+            device_id={"gx": x, "gy": y}, device_id_type=MESH,
+        ).start()
+
+    for near in (0, 2):
+        back_top = dot(turned, by[:, 128 * near : 128 * near + 256])
+        for q in range(HX):
+            for p in range(2):
+                u, v = part(back_top, q, p), part(back_top, HX + q, p)
+                y = 2 * (near + p)
+                back_out[pl.ds(4 * crossed(2 * q, y), 8), :] = jnp.where(left, u, swap(v)).astype(BF)
+                back_out[pl.ds(4 * crossed(2 * q, y + 1), 8), :] = jnp.where(left, swap(u), v).astype(BF)
+        each_below(range(2 * near, 2 * near + 4), send_back)
+    pltpu.make_async_copy(
+        back_out.at[slot(crossed(gx, gy))], back_home.at[slot(me)], recv_sem.at[gx // 2]
+    ).start()
 
     copies[6].wait()
     copies[7].wait()

time: 37 us -> 35.9 us (0.970)
  Pallas kernels: 36.3 us -> 35.2 us
    pallas_call x1, Pallas kernels: 34.6 us -> 33.5 us  [on_device(): pl.pallas_call(kernel, out_shape=(jax.ShapeDtypeStruct((1024, 512), F32),...]
where the time goes in v5:
time: 35.9 us; the launch traced here: 35.8 us
  Pallas kernels  35.2 us (98%)
  between operations  0.64 us (2%)
    pallas_call x1, Pallas kernels, on_device(): pl.pallas_call(kernel, out_shape=(jax.ShapeDtypeStruct((1024, 512), F32),...  33.5 us
    pallas_call x1, Pallas kernels, on_device(): pl.pallas_call(deliver, out_shape=(jax.ShapeDtypeStruct((1024, 512), F32)...  1.68 us

profile of v5, /device:TPU:1, one launch (start us, length us, event | category | flops | bytes accessed | tf_op | source)
XLA Modules:
  0.0 35.8 jit_solution(2459892041246258933)
XLA Ops:
  0.6 33.5 %shard_map.95 = (f32[1024,512]{1,0:T(8,128)S(1)}, bf16[1024,512]{1,0:T(8,128)(2,1)S(1)}) custom-call(bf16[1024,512]{1,0:T(8,128)(2,1)} %bitcast.9, bf16[1024,512]{1,0:T(8,128)(2,1)} %bitcast.10, f32[8,16]{1,0:T(8,128)} %thr.1, s32[128,256]{1,0:T(8,128)} %bitcast.12, bf16[64,512]{1,0:T(8,128)(2,1)} %bitcast.13, bf16[64,512]{1,0:T(8,128)(2,1)} %eb.1, ...), custom_call_target="tpu_custom_call" | custom-call | tf_op jit(solution)/shard_map/pallas_call | solution.py:302
  34.1 1.7 %shard_map.96 = (f32[1024,512]{1,0:T(8,128)}, bf16[1024,512]{1,0:T(8,128)(2,1)}) custom-call(f32[1024,512]{1,0:T(8,128)S(1)} %get-tuple-element.6.model_v, bf16[1024,512]{1,0:T(8,128)(2,1)S(1)} %get-tuple-element.7.residual_v), custom_call_target="tpu_custom_call" | custom-call | tf_op jit(solution)/shard_map/pallas_call | solution.py:349
